TPU v7x, 32 devices: a whole 2x2x4 slice. The times are simulated.
32 devices in a mesh: seq: 2 (over y), dom: 8 (over z, x), tm: 2 (over core).
Axes of the slice: x: 2, y: 2, z: 4, core: 2. Of those that a mesh axis runs over, the one named last changes fastest.
Arguments:
- particles: bfloat16 [4, 1536, 128], P('tm', ('seq', 'dom')), parts along dimension 1, may hold values from -6 to 6
- log_weight: float32 [4, 1536], P('tm', ('seq', 'dom')), parts along dimension 1, may hold values from -13 to 313
- trans_weight: bfloat16 [128, 128], replicated, may hold values from -0.5 to 0.5
- precision: float32 [128], replicated, may hold values from 0.2 to 2
Outputs:
- smoothed: float32 [4, 1536], P('tm', ('seq', 'dom')), parts along dimension 1
- score: float32 [256, 128], P('seq'), parts along dimension 0
There are 2 independent parts, one for each index of `seq`. A program takes and returns all parts, laid end to end along the dimension named above; an argument that names none is the same for every part. Nothing has to cross between parts.
All inputs are finite; a program needn't handle non-finite values.
Results may differ from a plain program's by a relative error of at most 0.0061.
Values may be sent and summed in bfloat16 or wider, within the bound.
A program may use at most 64 MiB of HBM per device.

v0:
```python
import jax
import jax.numpy as jnp
from jax import lax
from jax.sharding import PartitionSpec as P

exact_mode = lax.Precision.HIGHEST


def from_behind(x, axis, by):
    size = lax.axis_size(axis)
    pairs = [(i, i + by) for i in range(size) if 0 <= i + by < size]
    return lax.ppermute(x, axis, pairs)


def block_size(length):
    best = 1
    for trial in range(1, min(length, 512) + 1):
        if length % trial == 0:
            best = trial
    return best


def project_rows(rows, precision, weight_full):
    return jnp.dot(rows.astype(jnp.float32) * precision, weight_full, precision=exact_mode).astype(
        jnp.bfloat16
    )


def pair_scores(row_proj, column_rows, column_bias):
    return (
        jnp.einsum("id,jd->ij", row_proj, column_rows, preferred_element_type=jnp.float32)
        + column_bias[None, :]
    )


def make_norm_fold(row_proj, bias_row, carried, block_in, first_row):
    length = block_in.shape[0]
    size = block_size(length)

    def inner(position, state):
        row_top, row_total = state
        offset = position * size
        column_rows = lax.dynamic_slice_in_dim(block_in, offset, size, 0)
        bias_part = lax.dynamic_slice_in_dim(bias_row, first_row + offset, size, 0)
        scores = pair_scores(row_proj, column_rows, bias_part)
        new_top = jnp.maximum(row_top, jnp.max(scores, axis=1))
        row_total = row_total * jnp.exp(row_top - new_top) + jnp.sum(
            jnp.exp(scores - new_top[:, None]), axis=1
        )
        return (new_top, row_total)

    return lax.fori_loop(0, length // size, inner, carried)


def make_column_fold(row_proj, bias_row, row_norm, row_weight, carried, block_in, first_row):
    length = block_in.shape[0]
    size = block_size(length)

    def inner(position, state):
        moved, column_sums = state
        offset = position * size
        column_rows = lax.dynamic_slice_in_dim(block_in, offset, size, 0)
        bias_part = lax.dynamic_slice_in_dim(bias_row, first_row + offset, size, 0)
        scores = pair_scores(row_proj, column_rows, bias_part)
        backward = (row_weight[:, None] * jnp.exp(scores - row_norm[:, None])).astype(jnp.bfloat16)
        moved = moved + jnp.dot(backward, column_rows, preferred_element_type=jnp.float32)
        column_sums = lax.dynamic_update_slice_in_dim(
            column_sums, jnp.sum(backward.astype(jnp.float32), axis=0), first_row + offset, 0
        )
        return (moved, column_sums)

    return lax.fori_loop(0, length // size, inner, carried)


def shards(particles, log_weight, trans_weight, precision):
    steps_here, rows_here, width = particles.shape
    tm_count = lax.axis_size("tm")
    dom_count = lax.axis_size("dom")
    total_rows = rows_here * dom_count
    tm_place = lax.axis_index("tm")
    is_last = tm_place == tm_count - 1
    weight_full = trans_weight.astype(jnp.float32)
    boundary = from_behind(particles[0], "tm", -1)
    later_sets = [particles[1]] + [boundary]
    later_proj = [project_rows(rows, precision, weight_full) for rows in later_sets]
    biases = []
    for k in range(steps_here):
        predicted = jnp.dot(particles[k], trans_weight.T, preferred_element_type=jnp.float32)
        biases.append(log_weight[k] - 0.5 * jnp.sum(precision * predicted * predicted, axis=1))
    local_bias = jnp.stack(biases)
    full_bias = lax.all_gather(local_bias, "dom", axis=1, tiled=True)
    row_norms = []
    whole = lax.all_gather(particles, "dom", axis=1, tiled=True)
    for k in range(steps_here):
        start_state = (
            jnp.full((rows_here,), -jnp.inf, jnp.float32),
            jnp.zeros((rows_here,), jnp.float32),
        )
        row_top, row_total = make_norm_fold(later_proj[k], full_bias[k], start_state, whole[k], 0)
        row_norms.append(row_top + jnp.log(row_total))
    final_logs = log_weight[steps_here - 1]
    global_top = lax.pmax(jnp.max(final_logs), "dom")
    global_total = lax.psum(jnp.sum(jnp.exp(final_logs - global_top)), "dom")
    final_weights = jnp.exp(final_logs - global_top) / global_total
    carried = (
        jnp.zeros((steps_here, rows_here), jnp.float32),
        jnp.zeros((width, width), jnp.float32),
    )
    for r in range(tm_count):
        if r == 0:
            incoming = jnp.zeros((rows_here,), jnp.float32)
        else:
            incoming = from_behind(carried[0][0], "tm", -1)
        owner = tm_count - 1 - r
        backward_partial_value = jnp.zeros((width, width), jnp.float32)
        outputs = [None] * steps_here
        row_weight = incoming
        for backward_k in range(steps_here - 1, -1, -1):
            column_rows = particles[backward_k]
            backward_start_state = (
                jnp.zeros((rows_here, width), jnp.float32),
                jnp.zeros((total_rows,), jnp.float32),
            )
            moved, column_sums = make_column_fold(
                later_proj[backward_k],
                full_bias[backward_k],
                row_norms[backward_k],
                row_weight,
                backward_start_state,
                whole[backward_k],
                0,
            )
            column_weights = lax.psum_scatter(column_sums, "dom", scatter_dimension=0, tiled=True)
            outer = jnp.dot(
                later_sets[backward_k].astype(jnp.float32).T, moved, precision=exact_mode
            )
            column_float = column_rows.astype(jnp.float32)
            moment = jnp.dot(
                column_float.T * column_weights[None, :], column_float, precision=exact_mode
            )
            backward_partial_value = backward_partial_value + precision[:, None] * (
                outer - jnp.dot(weight_full, moment, precision=exact_mode)
            )
            if backward_k == steps_here - 1:
                column_weights = jnp.where(is_last, final_weights, column_weights)
            outputs[backward_k] = column_weights
            row_weight = column_weights
        is_owner = tm_place == owner
        carried = (
            jnp.where(is_owner, jnp.stack(outputs), carried[0]),
            jnp.where(is_owner, backward_partial_value, carried[1]),
        )
    stacked, partial_value = carried
    score = lax.psum(partial_value, ("dom", "tm"))
    return (stacked * total_rows, score)


def solution(mesh):
    placed = (P("tm", ("seq", "dom"), None), P("tm", ("seq", "dom")), P(), P())
    return jax.shard_map(
        shards,
        mesh=mesh,
        in_specs=placed,
        out_specs=(P("tm", ("seq", "dom")), P("seq", None)),
        check_vma=False,
    )
```

profile of v0, /device:TPU:8, one launch (start us, length us, event | category | flops | bytes accessed | tf_op | source)
XLA Modules:
  0.0 267.3 jit_solution(9784451875654501515)
XLA Ops:
  7.2 0.8 slice_bitcast_fusion.2
  8.0 1.4 collective-permute-start
  9.4 28.6 %all_gather.6 = bf16[2,768,128]{2,1,0:T(8,128)(2,1)S(1)} all-gather(bf16[2,96,128]{2,1,0:T(8,128)(2,1)S(1)} %copy-done.1), channel_id=1, replica_groups=mesh['seq'=2,'dom'=8,'tm'=2] {'dom'}, dimensions={1}, use_global_device_ids=true | all-gather | bytes 442368 | tf_op jit(solution)/shard_map/all_gather | solution.py:93
  38.0 0.3 fusion.54
  38.3 0.3 fusion.53
  38.8 0.6 copy-done.3
  39.4 0.6 slice_reduce_fusion.2
  40.0 22.1 %pmax.7 = f32[]{:T(128)} all-reduce(f32[]{:T(128)} %slice_reduce_fusion.2), channel_id=1, replica_groups=mesh['seq'=2,'dom'=8,'tm'=2] {'dom'}, use_global_device_ids=true, to_apply=%region_3.4 | all-reduce | flops 1 | bytes 8 | tf_op jit(solution)/shard_map/pmax | solution.py:102
  62.1 1.2 fusion.81
  63.3 16.3 %all-gather = f32[8,96,2]{1,2,0:T(2,128)S(1)} all-gather(f32[1,96,2]{1,2,0:T(2,128)S(1)} %maximum_bitcast_fusion), channel_id=1, replica_groups=mesh['seq'=2,'dom'=8,'tm'=2] {'dom'}, dimensions={0}, use_global_device_ids=true | all-gather | bytes 6912 | tf_op jit(solution)/shard_map/all_gather | solution.py:91
  79.7 1.2 while.98
  79.8 0.3 fusion.143
  80.1 0.2 exponential_reduce_fusion.5
  80.4 0.3 fusion.143
  80.7 0.2 exponential_reduce_fusion.5
  81.0 0.6 copy-done.4
  81.7 0.6 dynamic-slice
  83.1 1.2 while.96
  83.2 0.3 fusion.136
  83.4 0.2 exponential_reduce_fusion.4
  83.7 0.3 fusion.136
  84.0 0.2 exponential_reduce_fusion.4
  84.3 1.5 while.97
  84.4 0.2 convert_reduce_fusion.8
  84.8 0.2 dynamic_update_slice.36
  85.1 0.2 convert_reduce_fusion.8
  85.3 0.2 convolution_add_fusion.14
  85.5 0.2 dynamic_update_slice.36
  85.8 19.9 %all-reduce.4 = (f32[768]{0:T(1024)S(1)}, f32[]{:T(128)}) all-reduce(f32[768]{0:T(1024)S(1)} %get-tuple-element.769, f32[]{:T(128)} %get-tuple-element.1041), channel_id=2, replica_groups=mesh['seq'=2,'dom'=8,'tm'=2] {'dom'}, use_global_device_ids=true, to_apply=%region_13.0.clone | all-reduce | flops 769 | bytes 6152
  105.6 1.3 broadcast_select_fusion.5
  106.9 1.5 while.99
  107.0 0.2 convert_reduce_fusion.9
  107.4 0.2 dynamic_update_slice.37
  107.7 0.2 convert_reduce_fusion.9
  108.1 0.2 dynamic_update_slice.37
  108.4 17.1 %all-reduce.1 = f32[768]{0:T(1024)S(1)} all-reduce(f32[768]{0:T(1024)S(1)} %get-tuple-element.772), channel_id=3, replica_groups=mesh['seq'=2,'dom'=8,'tm'=2] {'dom'}, use_global_device_ids=true, to_apply=%region_21.22.clone | all-reduce | flops 768 | bytes 6144
  125.6 1.3 collective-permute-start.1
  126.9 0.2 fusion.57
  127.2 0.3 fusion.52
  127.5 0.3 fusion.50
  127.8 0.2 fusion.86
  128.1 0.2 convolution_subtract_fusion
  128.3 0.3 fusion.44
  128.7 1.5 while.100
  128.7 0.2 convert_reduce_fusion.10
  129.1 0.2 dynamic_update_slice.38
  129.5 0.2 convert_reduce_fusion.10
  129.9 0.2 dynamic_update_slice.38
  130.1 19.1 %all-reduce.2 = f32[768]{0:T(1024)S(1)} all-reduce(f32[768]{0:T(1024)S(1)} %get-tuple-element.773), channel_id=4, replica_groups=mesh['seq'=2,'dom'=8,'tm'=2] {'dom'}, use_global_device_ids=true, to_apply=%region_25.26.clone | all-reduce | flops 768 | bytes 6144
  149.3 1.5 while.101
  149.4 0.2 convert_reduce_fusion.11
  149.8 0.2 dynamic_update_slice.39
  150.1 0.2 convert_reduce_fusion.11
  150.5 0.2 dynamic_update_slice.39
  150.8 17.1 %all-reduce.3 = f32[768]{0:T(1024)S(1)} all-reduce(f32[768]{0:T(1024)S(1)} %get-tuple-element.774), channel_id=5, replica_groups=mesh['seq'=2,'dom'=8,'tm'=2] {'dom'}, use_global_device_ids=true, to_apply=%region_29.30.clone | all-reduce | flops 768 | bytes 6144
  168.0 0.2 fusion.60
  168.3 0.3 fusion.51
  168.6 0.3 fusion.49
  168.9 0.2 fusion.85
  169.2 0.2 convolution_subtract_fusion.2
  169.4 0.9 fusion.48
  170.4 0.6 fusion.80
  170.9 88.0 %all-reduce.7.cloned.1.call-done = f32[128,128]{0,1:T(8,128)} async-done(((f32[128,128]{0,1:T(8,128)}), f32[128,128]{0,1:T(8,128)}) %all-reduce.7.cloned.1.call-update) | async-done | bytes 65552 | tf_op jit(solution)/shard_map/psum | solution.py:154
  258.9 1.6 copy.10
  (70 shorter events, 3.3 us)
Async XLA Ops:
  7.2 30.9 %copy-start = (bf16[128,128]{1,0:T(8,128)(2,1)S(1)}, bf16[128,128]{1,0:T(8,128)(2,1)}, u32[]{:S(2)}) copy-start(bf16[128,128]{1,0:T(8,128)(2,1)} %param.18) | copy-start | bytes 98308
  7.2 2.2 copy-start.1
  7.2 251.7 %all-reduce.7.cloned.1.call-start = ((), (), s32[]{:S(2)}) async-start(), calls=%async_computation | async-start | bytes 131072 | tf_op jit(solution)/shard_map/psum | solution.py:154
  8.0 30.0 %copy-start.2 = (f32[128]{0:T(128)S(1)}, f32[128]{0:T(128)}, u32[]{:S(2)}) copy-start(f32[128]{0:T(128)} %param.19) | copy-start | bytes 1540
  8.0 74.9 %collective-permute-start = (bf16[96,128]{1,0:T(8,128)(2,1)S(1)}, bf16[96,128]{1,0:T(8,128)(2,1)S(1)}, u32[]{:S(2)}, u32[]{:S(2)}) collective-permute-start(bf16[96,128]{1,0:T(8,128)(2,1)S(1)} %slice_bitcast_fusion.2), channel_id=1, source_target_pairs={{1,0},{3,2},{5,4},{7,6},{9,8},{11,10},{13,12},{15,14},{17,16},{19,... | collective-permute-start | bytes 73736 | tf_op jit(solution)/shard_map/ppermute | solution.py:12
  38.7 0.7 copy-start.3
  81.0 0.7 copy-start.4
  125.6 3.0 %collective-permute-start.1 = (f32[96]{0:T(128)S(1)}, f32[96]{0:T(128)S(1)}, u32[]{:S(2)}, u32[]{:S(2)}) collective-permute-start(f32[96]{0:T(128)S(1)} %slice_bitcast_fusion.3), channel_id=1, source_target_pairs={{1,0},{3,2},{5,4},{7,6},{9,8},{11,10},{13,12},{15,14},{17,16},{19,... | collective-permute-start | bytes 1160 | tf_op jit(solution)/shard_map/ppermute | solution.py:12
Sparse Core Ops, SparseCore 0:
  170.5 88.4 all-reduce.6
where the time goes:
time: 268 us; the launch traced here: 267 us
  blocking collectives  140 us (52%)
  waiting for transfers between devices  88.1 us (33%)
  between operations  14.9 us (6%)
  matrix products  8.92 us (3%)
  local copies, waits for them, and re-layouts  7.58 us (3%)
  other arithmetic  4.58 us (2%)
  starting transfers between devices  2.74 us (1%)
    psum x1, waiting for transfers between devices, shards(): score = lax.psum(partial_value, ('dom', 'tm'))  88 us
    unnamed x4, blocking collectives  73.2 us
    all_gather x1, blocking collectives, shards(): whole = lax.all_gather(particles, 'dom', axis=1, tiled=True)  28.6 us
    pmax x1, blocking collectives, shards(): global_top = lax.pmax(jnp.max(final_logs), 'dom')  22.1 us
    all_gather x1, blocking collectives, shards(): full_bias = lax.all_gather(local_bias, 'dom', axis=1, tiled=True)  16.3 us
  transfers between devices with their start and end apart: 3, of which 2 were waited for; matrix products, arithmetic and copies ran while one was open for 2% of the time, Pallas kernels for 0%

commit v1 on v0

--- a/solution.py
+++ b/solution.py
@@ -151,7 +151,9 @@
             jnp.where(is_owner, backward_partial_value, carried[1]),
         )
     stacked, partial_value = carried
-    score = lax.psum(partial_value, ("dom", "tm"))
+    score = partial_value
+    for over in ("tm", "dom"):
+        score = lax.psum(score, over)
     return (stacked * total_rows, score)
 
 

time: 268 us -> 273 us (1.019)
  waiting for transfers between devices: 88.1 us -> 92 us
    psum x1 -> x2, waiting for transfers between devices: 88 us -> 91.9 us  [shards(): score = lax.psum(score, over)]
  transfers between devices with their start and end apart: 3 -> 4, of which waited for: 2 -> 3; matrix products, arithmetic and copies ran while one was open for 2% -> 2% of each run, Pallas kernels for 0% -> 0%
where the time goes in v1:
time: 273 us; the launch traced here: 271 us
  blocking collectives  140 us (51%)
  waiting for transfers between devices  92 us (34%)
  between operations  14.9 us (5%)
  matrix products  8.93 us (3%)
  local copies, waits for them, and re-layouts  7.58 us (3%)
  other arithmetic  4.58 us (2%)
  starting transfers between devices  2.78 us (1%)
    psum x2, waiting for transfers between devices, shards(): score = lax.psum(score, over)  91.9 us
    unnamed x4, blocking collectives  73.2 us
    all_gather x1, blocking collectives, shards(): whole = lax.all_gather(particles, 'dom', axis=1, tiled=True)  28.6 us
    pmax x1, blocking collectives, shards(): global_top = lax.pmax(jnp.max(final_logs), 'dom')  22.1 us
    all_gather x1, blocking collectives, shards(): full_bias = lax.all_gather(local_bias, 'dom', axis=1, tiled=True)  16.3 us
  transfers between devices with their start and end apart: 4, of which 3 were waited for; matrix products, arithmetic and copies ran while one was open for 2% of the time, Pallas kernels for 0%

profile of v1, /device:TPU:8, one launch (start us, length us, event | category | flops | bytes accessed | tf_op | source)
XLA Modules:
  0.0 271.3 jit_solution(8518882286427378207)
XLA Ops:
  7.2 0.8 slice_bitcast_fusion.2
  8.0 1.4 collective-permute-start
  9.4 28.6 %all_gather.6 = bf16[2,768,128]{2,1,0:T(8,128)(2,1)S(1)} all-gather(bf16[2,96,128]{2,1,0:T(8,128)(2,1)S(1)} %copy-done.1), channel_id=1, replica_groups=mesh['seq'=2,'dom'=8,'tm'=2] {'dom'}, dimensions={1}, use_global_device_ids=true | all-gather | bytes 442368 | tf_op jit(solution)/shard_map/all_gather | solution.py:93
  38.0 0.3 fusion.54
  38.3 0.3 fusion.53
  38.8 0.6 copy-done.3
  39.4 0.6 slice_reduce_fusion.2
  40.0 22.1 %pmax.7 = f32[]{:T(128)} all-reduce(f32[]{:T(128)} %slice_reduce_fusion.2), channel_id=1, replica_groups=mesh['seq'=2,'dom'=8,'tm'=2] {'dom'}, use_global_device_ids=true, to_apply=%region_3.4 | all-reduce | flops 1 | bytes 8 | tf_op jit(solution)/shard_map/pmax | solution.py:102
  62.1 1.2 fusion.81
  63.3 16.3 %all-gather = f32[8,96,2]{1,2,0:T(2,128)S(1)} all-gather(f32[1,96,2]{1,2,0:T(2,128)S(1)} %maximum_bitcast_fusion), channel_id=1, replica_groups=mesh['seq'=2,'dom'=8,'tm'=2] {'dom'}, dimensions={0}, use_global_device_ids=true | all-gather | bytes 6912 | tf_op jit(solution)/shard_map/all_gather | solution.py:91
  79.7 1.2 while.98
  79.8 0.3 fusion.143
  80.1 0.2 exponential_reduce_fusion.5
  80.4 0.3 fusion.143
  80.7 0.2 exponential_reduce_fusion.5
  81.0 0.6 copy-done.4
  81.7 0.6 dynamic-slice
  83.1 1.2 while.96
  83.2 0.3 fusion.136
  83.4 0.2 exponential_reduce_fusion.4
  83.7 0.3 fusion.136
  84.0 0.2 exponential_reduce_fusion.4
  84.3 1.5 while.97
  84.4 0.2 convert_reduce_fusion.8
  84.8 0.2 dynamic_update_slice.36
  85.1 0.2 convert_reduce_fusion.8
  85.5 0.2 dynamic_update_slice.36
  85.8 19.9 %all-reduce.4 = (f32[768]{0:T(1024)S(1)}, f32[]{:T(128)}) all-reduce(f32[768]{0:T(1024)S(1)} %get-tuple-element.769, f32[]{:T(128)} %get-tuple-element.1041), channel_id=2, replica_groups=mesh['seq'=2,'dom'=8,'tm'=2] {'dom'}, use_global_device_ids=true, to_apply=%region_13.0.clone | all-reduce | flops 769 | bytes 6152
  105.6 1.3 broadcast_select_fusion.5
  106.9 1.5 while.99
  107.0 0.2 convert_reduce_fusion.9
  107.4 0.2 dynamic_update_slice.37
  107.7 0.2 convert_reduce_fusion.9
  108.1 0.2 dynamic_update_slice.37
  108.4 17.1 %all-reduce.1 = f32[768]{0:T(1024)S(1)} all-reduce(f32[768]{0:T(1024)S(1)} %get-tuple-element.772), channel_id=3, replica_groups=mesh['seq'=2,'dom'=8,'tm'=2] {'dom'}, use_global_device_ids=true, to_apply=%region_21.22.clone | all-reduce | flops 768 | bytes 6144
  125.6 1.3 collective-permute-start.1
  126.9 0.2 fusion.57
  127.2 0.3 fusion.52
  127.5 0.3 fusion.50
  127.8 0.2 fusion.86
  128.1 0.2 convolution_subtract_fusion
  128.3 0.3 fusion.44
  128.7 1.5 while.100
  128.7 0.2 convert_reduce_fusion.10
  129.1 0.2 dynamic_update_slice.38
  129.5 0.2 convert_reduce_fusion.10
  129.9 0.2 dynamic_update_slice.38
  130.1 19.1 %all-reduce.2 = f32[768]{0:T(1024)S(1)} all-reduce(f32[768]{0:T(1024)S(1)} %get-tuple-element.773), channel_id=4, replica_groups=mesh['seq'=2,'dom'=8,'tm'=2] {'dom'}, use_global_device_ids=true, to_apply=%region_25.26.clone | all-reduce | flops 768 | bytes 6144
  149.3 1.5 while.101
  149.4 0.2 convert_reduce_fusion.11
  149.8 0.2 dynamic_update_slice.39
  150.1 0.2 convert_reduce_fusion.11
  150.5 0.2 dynamic_update_slice.39
  150.8 17.1 %all-reduce.3 = f32[768]{0:T(1024)S(1)} all-reduce(f32[768]{0:T(1024)S(1)} %get-tuple-element.774), channel_id=5, replica_groups=mesh['seq'=2,'dom'=8,'tm'=2] {'dom'}, use_global_device_ids=true, to_apply=%region_29.30.clone | all-reduce | flops 768 | bytes 6144
  167.9 0.2 fusion.60
  168.2 0.3 fusion.51
  168.5 0.3 fusion.49
  168.9 0.2 fusion.85
  169.1 0.2 convolution_subtract_fusion.2
  169.4 0.9 fusion.48
  170.4 19.5 %all-reduce.8.cloned.1.call-done = f32[128,128]{0,1:T(8,128)} async-done(((f32[128,128]{0,1:T(8,128)}), f32[128,128]{0,1:T(8,128)}) %all-reduce.8.cloned.1.call-update) | async-done | bytes 65552 | tf_op jit(solution)/shard_map/psum | solution.py:156
  189.9 0.6 fusion.80
  190.5 72.4 %all-reduce.10.cloned.1.call-done = f32[128,128]{0,1:T(8,128)} async-done(((f32[128,128]{0,1:T(8,128)}), f32[128,128]{0,1:T(8,128)}) %all-reduce.10.cloned.1.call-update) | async-done | bytes 65552 | tf_op jit(solution)/shard_map/psum | solution.py:156
  262.9 1.6 copy.10
  (73 shorter events, 3.5 us)
Async XLA Ops:
  7.2 30.9 %copy-start = (bf16[128,128]{1,0:T(8,128)(2,1)S(1)}, bf16[128,128]{1,0:T(8,128)(2,1)}, u32[]{:S(2)}) copy-start(bf16[128,128]{1,0:T(8,128)(2,1)} %param.18) | copy-start | bytes 98308
  7.2 2.2 copy-start.1
  7.2 182.7 %all-reduce.8.cloned.1.call-start = ((), (), s32[]{:S(2)}) async-start(), calls=%async_computation | async-start | bytes 131072 | tf_op jit(solution)/shard_map/psum | solution.py:156
  8.0 30.0 %copy-start.2 = (f32[128]{0:T(128)S(1)}, f32[128]{0:T(128)}, u32[]{:S(2)}) copy-start(f32[128]{0:T(128)} %param.19) | copy-start | bytes 1540
  8.0 74.9 %collective-permute-start = (bf16[96,128]{1,0:T(8,128)(2,1)S(1)}, bf16[96,128]{1,0:T(8,128)(2,1)S(1)}, u32[]{:S(2)}, u32[]{:S(2)}) collective-permute-start(bf16[96,128]{1,0:T(8,128)(2,1)S(1)} %slice_bitcast_fusion.2), channel_id=1, source_target_pairs={{1,0},{3,2},{5,4},{7,6},{9,8},{11,10},{13,12},{15,14},{17,16},{19,... | collective-permute-start | bytes 73736 | tf_op jit(solution)/shard_map/ppermute | solution.py:12
  38.7 0.7 copy-start.3
  81.0 0.7 copy-start.4
  125.6 3.0 %collective-permute-start.1 = (f32[96]{0:T(128)S(1)}, f32[96]{0:T(128)S(1)}, u32[]{:S(2)}, u32[]{:S(2)}) collective-permute-start(f32[96]{0:T(128)S(1)} %slice_bitcast_fusion.3), channel_id=1, source_target_pairs={{1,0},{3,2},{5,4},{7,6},{9,8},{11,10},{13,12},{15,14},{17,16},{19,... | collective-permute-start | bytes 1160 | tf_op jit(solution)/shard_map/ppermute | solution.py:12
  170.3 92.6 %all-reduce.10.cloned.1.call-start = ((), (), s32[]{:S(2)}) async-start(), calls=%async_computation.1 | async-start | bytes 131072 | tf_op jit(solution)/shard_map/psum | solution.py:156
Sparse Core Ops, SparseCore 0:
  170.4 19.4 all-reduce.7
  193.3 69.5 all-reduce.9
